TPU v7x, 256 devices: a whole 4x4x8 slice. The times are simulated.
256 devices in a mesh: replica: 16 (over z_hi, x), dp: 2 (over core), shard: 8 (over y, z_lo).
Axes of the slice: x: 4, y: 4, z: 8 (z_hi: 4, z_lo: 2; z = z_hi * 2 + z_lo), core: 2. Of those that a mesh axis runs over, the one named last changes fastest.
Arguments:
- round_index: int32 [2], replicated, may hold values from 0 to 2999
- activations: bfloat16 [2, 16, 2048, 4096], P(None, 'replica', ('dp', 'shard')), may hold values from -6 to 6
- cotangents: bfloat16 [2, 16, 2048, 2048], P(None, 'replica', 'dp', 'shard'), may hold values from -0.119628906 to 0.119628906
- params: float32 [16, 4096, 2048], P('replica', 'dp', 'shard'), may hold values from -6 to 6
- momentum: float32 [16, 4096, 2048], P('replica', 'dp', 'shard'), may hold values from -3 to 3
Outputs:
- new_params: float32 [16, 4096, 2048], P('replica', 'dp', 'shard')
- new_momentum: float32 [16, 4096, 2048], P('replica', 'dp', 'shard')
All inputs are finite; a program needn't handle non-finite values.
Results may differ from a plain program's by a relative error of at most 0.0003.
Values may be sent and summed in bfloat16 or wider, within the bound.
A program may use at most 128 MiB of HBM per device.

v0:
```python
from functools import partial

import jax
import jax.numpy as jnp
from jax import lax
from jax.sharding import PartitionSpec as P

ROUNDS = 2


momentum_coef = 0.9
step_size = 0.25


def swapped(block, axis, stride):
    count = lax.axis_size(axis)
    route = []
    for low in range(count):
        high = low | 1 << stride
        if high != low and high < count:
            route += [(low, high), (high, low)]
    return lax.ppermute(block, axis, route)


def contract(piece, cot_all):
    return lax.dot_general(
        piece, cot_all, (((0,), (0,)), ((), ())), preferred_element_type=jnp.float32
    )


def gradient(activations, cotangents, k):
    tok_rows = activations[k, 0]
    cot_block = cotangents[k, 0]
    summed = contract(lax.all_gather(tok_rows, "shard", axis=0, tiled=True), cot_all=cot_block)
    return lax.psum_scatter(summed, "dp", scatter_dimension=0, tiled=True)


def trade_with(level, values):
    return swapped(values, "replica", level)


def advance(round_index, k, grad, params_now, moment_now):
    moment_next = momentum_coef * moment_now + grad
    stepped = params_now - step_size * (grad + momentum_coef * moment_next)
    branches = [partial(trade_with, level) for level in range(3)]
    partner = lax.switch(round_index[k] % 3, branches, stepped)
    return ((stepped + partner) * 0.5, moment_next)


def local(round_index, activations, cotangents, params, momentum):
    params_now = params[0]
    moment_now = momentum[0]
    for k in range(ROUNDS):
        grad = gradient(activations, cotangents, k)
        params_now, moment_now = advance(round_index, k, grad, params_now, moment_now)
    return (params_now[None], moment_now[None])


def solution(mesh):
    in_specs = (
        P(),
        P(None, "replica", ("dp", "shard"), None),
        P(None, "replica", "dp", "shard"),
        P("replica", "dp", "shard"),
        P("replica", "dp", "shard"),
    )
    out_specs = (P("replica", "dp", "shard"), P("replica", "dp", "shard"))
    return jax.shard_map(local, mesh=mesh, in_specs=in_specs, out_specs=out_specs, check_vma=False)
```

profile of v0, /device:TPU:1, one launch (start us, length us, event | category | flops | bytes accessed | tf_op | source)
XLA Modules:
  0.0 539.8 jit_solution(17033155358475659714)
XLA Ops:
  7.2 0.0 all-gather.5.cloned.1.call-start
  7.2 3.1 fusion.11
  10.3 0.0 copy-start.2
  10.3 0.0 all-gather.5.cloned.1.call-update
  10.3 0.0 all-gather.7.cloned.1.call-start
  10.4 0.7 all-gather.7.cloned.1.call-update
  11.1 0.0 reduce-scatter.3.cloned.1.call-start
  11.1 173.9 %all-gather.5.cloned.1.call-done = bf16[1,1,1024,4096]{3,2,1,0:T(8,128)(2,1)} async-done(((bf16[1,1,128,4096]{3,2,1,0:T(8,128)(2,1)}), bf16[1,1,1024,4096]{3,2,1,0:T(8,128)(2,1)}) %all-gather.5.cloned.1.call-update) | async-done | bytes 8388624 | tf_op jit(solution)/shard_map/all_gather | solution.py:34
  185.0 0.0 copy-done.2
  185.0 7.8 %fusion.2 = f32[4096,256]{1,0:T(8,128)} fusion(bf16[1,1,1024,4096]{3,2,1,0:T(8,128)(2,1)} %all-gather.5.cloned.1.call-done, bf16[2,1,1024,256]{3,2,1,0:T(8,128)(2,1)S(1)} %copy-done.2), kind=kOutput, calls=%fused_computation.2 | convolution fusion | flops 2147483648 | bytes 13107200 | tf_op jit(solution)/shard_map/dot_general | solution.py:26
  192.8 0.0 reduce-scatter.3.cloned.1.call-update
  192.8 0.0 reduce-scatter.5.cloned.1.call-start
  192.9 166.4 %all-gather.7.cloned.1.call-done = bf16[1,1,1024,4096]{3,2,1,0:T(8,128)(2,1)} async-done(((bf16[1,1,128,4096]{3,2,1,0:T(8,128)(2,1)}), bf16[1,1,1024,4096]{3,2,1,0:T(8,128)(2,1)}) %all-gather.7.cloned.1.call-update) | async-done | bytes 8388624 | tf_op jit(solution)/shard_map/all_gather | solution.py:34
  359.3 7.8 %fusion = f32[4096,256]{1,0:T(8,128)} fusion(bf16[1,1,1024,4096]{3,2,1,0:T(8,128)(2,1)} %all-gather.7.cloned.1.call-done, bf16[2,1,1024,256]{3,2,1,0:T(8,128)(2,1)S(1)} %copy-done.2), kind=kOutput, calls=%fused_computation | convolution fusion | flops 2147483648 | bytes 13107200 | tf_op jit(solution)/shard_map/dot_general | solution.py:26
  367.1 0.0 copy-start.1
  367.1 0.0 copy-start
  367.1 0.0 reduce-scatter.5.cloned.1.call-update
  367.1 0.6 copy-done.1
  367.7 0.6 fusion.12
  369.6 11.4 %reduce-scatter.3.cloned.1.call-done = f32[2048,256]{1,0:T(8,128)} async-done(((f32[4096,256]{1,0:T(8,128)}), f32[2048,256]{1,0:T(8,128)}) %reduce-scatter.3.cloned.1.call-update) | async-done | bytes 2097168 | tf_op jit(solution)/shard_map/reduce_scatter | solution.py:35
  381.1 0.0 copy-done
  381.1 2.7 bitcast_subtract_fusion
  383.8 47.1 %conditional.2 = (f32[2048,256]{1,0:T(8,128)}) conditional(s32[]{:T(128)} %clamp.6, f32[2048,256]{1,0:T(8,128)S(1)} %bitcast_subtract_fusion, f32[2048,256]{1,0:T(8,128)S(1)} %bitcast_subtract_fusion, f32[2048,256]{1,0:T(8,128)S(1)} %bitcast_subtract_fusion), branch_computations={%region_1.2_spmd, %region_2.3_spmd, %region_3.4_spmd} | conditional | bytes 8388656 | solution.py:46
  383.8 0.9 collective-permute-start
  384.7 46.2 %collective-permute-done = f32[2048,256]{1,0:T(8,128)} collective-permute-done((f32[2048,256]{1,0:T(8,128)S(1)}, f32[2048,256]{1,0:T(8,128)}, u32[]{:S(2)}, u32[]{:S(2)}) %collective-permute-start) | collective-permute-done | bytes 2097184 | tf_op jit(solution)/shard_map/cond/branch_0_fun/ppermute | solution.py:22
  430.9 0.0 reduce-scatter.5.cloned.1.call-done
  430.9 6.3 %fusion.6 = (f32[1,2048,256]{2,1,0:T(8,128)}, f32[2048,256]{1,0:T(8,128)S(1)}) fusion(f32[2048,256]{1,0:T(8,128)} %reduce-scatter.5.cloned.1.call-done, f32[2048,256]{1,0:T(8,128)} %reduce-scatter.3.cloned.1.call-done, f32[1,2048,256]{2,1,0:T(8,128)} %param.15, f32[2048,256]{1,0:T(8,128)} %get-tuple-element.22, f32[1,2048,256]{2,1,0:T(8,128)} %param.14), kind=kLoop, calls=%fused_computation.10 | loop fusion | flops 6815744 | bytes 14680064 | tf_op jit(solution)/shard_map/broadcast_in_dim | solution.py:56
  437.2 92.9 %conditional.3 = (f32[2048,256]{1,0:T(8,128)}) conditional(s32[]{:T(128)} %clamp.7, f32[2048,256]{1,0:T(8,128)S(1)} %get-tuple-element.17, f32[2048,256]{1,0:T(8,128)S(1)} %get-tuple-element.17, f32[2048,256]{1,0:T(8,128)S(1)} %get-tuple-element.17), branch_computations={%region_5.6_spmd, %region_6.7_spmd, %region_7.8_spmd} | conditional | bytes 8388656 | solution.py:46
  437.2 1.8 collective-permute-start.5
  439.0 91.1 %collective-permute-done.5 = f32[2048,256]{1,0:T(8,128)} collective-permute-done((f32[2048,256]{1,0:T(8,128)S(1)}, f32[2048,256]{1,0:T(8,128)}, u32[]{:S(2)}, u32[]{:S(2)}) %collective-permute-start.5) | collective-permute-done | bytes 2097184 | tf_op jit(solution)/shard_map/cond/branch_2_fun/ppermute | solution.py:22
  530.1 3.2 multiply_bitcast_fusion
Async XLA Ops:
  7.2 177.9 %all-gather.5.cloned.1.call-start = ((), (), s32[]{:S(2)}) async-start(), calls=%async_computation.4 | async-start | bytes 9437184 | tf_op jit(solution)/shard_map/all_gather | solution.py:34
  10.3 174.7 %copy-start.2 = (bf16[2,1,1024,256]{3,2,1,0:T(8,128)(2,1)S(1)}, bf16[2,1,1024,256]{3,2,1,0:T(8,128)(2,1)}, u32[]{:S(2)}) copy-start(bf16[2,1,1024,256]{3,2,1,0:T(8,128)(2,1)} %param.13) | copy-start | bytes 3145732
  10.3 348.9 %all-gather.7.cloned.1.call-start = ((), (), s32[]{:S(2)}) async-start(), calls=%async_computation.5 | async-start | bytes 9437184 | tf_op jit(solution)/shard_map/all_gather | solution.py:34
  11.1 370.0 %reduce-scatter.3.cloned.1.call-start = ((), (), s32[]{:S(2)}) async-start(), calls=%async_computation.2 | async-start | bytes 6291456 | tf_op jit(solution)/shard_map/reduce_scatter | solution.py:35
  192.8 238.1 %reduce-scatter.5.cloned.1.call-start = ((), (), s32[]{:S(2)}) async-start(), calls=%async_computation.3 | async-start | bytes 6291456 | tf_op jit(solution)/shard_map/reduce_scatter | solution.py:35
  367.1 0.7 copy-start.1
  367.1 14.0 %copy-start = (f32[1,2048,256]{2,1,0:T(8,128)S(1)}, f32[1,2048,256]{2,1,0:T(8,128)}, u32[]{:S(2)}) copy-start(f32[1,2048,256]{2,1,0:T(8,128)} %param.15) | copy-start | bytes 6291460
  383.8 47.1 %collective-permute-start = (f32[2048,256]{1,0:T(8,128)S(1)}, f32[2048,256]{1,0:T(8,128)}, u32[]{:S(2)}, u32[]{:S(2)}) collective-permute-start(f32[2048,256]{1,0:T(8,128)S(1)} %param), channel_id=1, source_target_pairs={{0,16},{16,0},{32,48},{48,32},{64,80},{80,64},{96,112},{112,96},{1... | collective-permute-start | bytes 6291464 | tf_op jit(solution)/shard_map/cond/branch_0_fun/ppermute | solution.py:22
  437.2 92.9 %collective-permute-start.5 = (f32[2048,256]{1,0:T(8,128)S(1)}, f32[2048,256]{1,0:T(8,128)}, u32[]{:S(2)}, u32[]{:S(2)}) collective-permute-start(f32[2048,256]{1,0:T(8,128)S(1)} %param.5), channel_id=1, source_target_pairs={{0,64},{64,0},{16,80},{80,16},{32,96},{96,32},{48,112},{112,48},{1... | collective-permute-start | bytes 6291464 | tf_op jit(solution)/shard_map/cond/branch_2_fun/ppermute | solution.py:22
Sparse Core Ops, SparseCore 0:
  10.4 174.5 all-gather.4
  187.4 171.8 all-gather.6
  361.8 19.2 reduce-scatter.2
  383.5 18.7 reduce-scatter.4
where the time goes:
time: 540 us
  waiting for transfers between devices  490 us (91%)
  matrix products  15.6 us (3%)
  between operations  15.1 us (3%)
  other arithmetic  12.1 us (2%)
    all_gather x2, waiting for transfers between devices, gradient(): lax.all_gather(tok_rows, 'shard', axis=0, tiled=True)  340 us
    ppermute x2, waiting for transfers between devices, swapped(): return lax.ppermute(block, axis, route)  137 us
    dot_general x2, matrix products, contract(): lax.dot_general(piece, cot_all, (((0,), (0,)), ((), ())), preferred_eleme...  15.6 us
    reduce_scatter x2, waiting for transfers between devices, gradient(): return lax.psum_scatter(summed, 'dp', scatter_dimension=0, tiled=True)  11.4 us
  transfers between devices with their start and end apart: 6, of which 5 were waited for; matrix products, arithmetic and copies ran while one was open for 3% of the time, Pallas kernels for 0%

commit v1 on v0

--- a/solution.py
+++ b/solution.py
@@ -22,20 +22,86 @@
     return lax.ppermute(block, axis, route)
 
 
-def contract(piece, cot_all):
-    return lax.dot_general(
-        piece, cot_all, (((0,), (0,)), ((), ())), preferred_element_type=jnp.float32
-    )
+def shifted(block, axis, route_of):
+    count = lax.axis_size(axis)
+    return lax.ppermute(block, axis, [(i, route_of(i)) for i in range(count)])
+
+
+def gather_tokens(rows):
+    count = lax.axis_size("shard")
+    ny = count // 2
+    half = rows.shape[0] // 2
+
+    def move(y_step, z_flip):
+        def route_of(s):
+            y, z = divmod(s, 2)
+            return ((y + y_step) % ny) * 2 + (z ^ z_flip)
+        return route_of
+
+    z_in = shifted(rows, "shard", move(0, 1))
+    from_dn = shifted(rows, "shard", move(1, 0))
+    from_up = shifted(rows, "shard", move(-1, 0))
+    z_from_dn = shifted(z_in, "shard", move(1, 0))
+    z_from_up = shifted(z_in, "shard", move(-1, 0))
+    far_a = shifted(from_dn[:half], "shard", move(1, 0))
+    far_b = shifted(from_up[half:], "shard", move(-1, 0))
+    z_far_a = shifted(z_from_dn[:half], "shard", move(1, 0))
+    z_far_b = shifted(z_from_up[half:], "shard", move(-1, 0))
+    blocks = [rows, z_in, from_dn, z_from_dn, from_up, z_from_up,
+              jnp.concatenate([far_a, far_b]), jnp.concatenate([z_far_a, z_far_b])]
+    s = lax.axis_index("shard")
+    y, z = s // 2, s % 2
+    sources = [
+        s,
+        y * 2 + (1 - z),
+        ((y - 1) % ny) * 2 + z,
+        ((y - 1) % ny) * 2 + (1 - z),
+        ((y + 1) % ny) * 2 + z,
+        ((y + 1) % ny) * 2 + (1 - z),
+        ((y + 2) % ny) * 2 + z,
+        ((y + 2) % ny) * 2 + (1 - z),
+    ]
+    return jnp.concatenate(blocks), sources
 
 
 def gradient(activations, cotangents, k):
     tok_rows = activations[k, 0]
     cot_block = cotangents[k, 0]
-    summed = contract(lax.all_gather(tok_rows, "shard", axis=0, tiled=True), cot_all=cot_block)
-    return lax.psum_scatter(summed, "dp", scatter_dimension=0, tiled=True)
+    block = tok_rows.shape[0]
+    gathered, sources = gather_tokens(tok_rows)
+    cot_rel = jnp.concatenate(
+        [lax.dynamic_slice_in_dim(cot_block, src * block, block, axis=0) for src in sources]
+    )
+    d = lax.axis_index("dp")
+    n_rows = tok_rows.shape[1] // 2
+    other = lax.dynamic_slice_in_dim(gathered, (1 - d) * n_rows, n_rows, axis=1)
+    mine = lax.dynamic_slice_in_dim(gathered, d * n_rows, n_rows, axis=1)
+    dims = (((0,), (0,)), ((), ()))
+    part_other = lax.dot_general(other, cot_rel, dims, preferred_element_type=jnp.float32)
+    sent = lax.ppermute(part_other, "dp", [(0, 1), (1, 0)])
+    part_mine = lax.dot_general(mine, cot_rel, dims, preferred_element_type=jnp.float32)
+    return part_mine + sent
+
+
+def trade_far(values):
+    count = lax.axis_size("replica")
+    nx = 4
+    half = values.shape[0] // 2
+
+    def hop(step):
+        def route_of(r):
+            zh, x = divmod(r, nx)
+            return zh * nx + (x + step) % nx
+        return route_of
+
+    a = shifted(shifted(values[:half], "replica", hop(1)), "replica", hop(1))
+    b = shifted(shifted(values[half:], "replica", hop(-1)), "replica", hop(-1))
+    return jnp.concatenate([a, b])
 
 
 def trade_with(level, values):
+    if level == 1:
+        return trade_far(values)
     return swapped(values, "replica", level)
 
 
@@ -50,9 +116,9 @@
 def local(round_index, activations, cotangents, params, momentum):
     params_now = params[0]
     moment_now = momentum[0]
+    grads = [gradient(activations, cotangents, k) for k in range(ROUNDS)]
     for k in range(ROUNDS):
-        grad = gradient(activations, cotangents, k)
-        params_now, moment_now = advance(round_index, k, grad, params_now, moment_now)
+        params_now, moment_now = advance(round_index, k, grads[k], params_now, moment_now)
     return (params_now[None], moment_now[None])
 
 

time: 540 us -> 338 us (0.63)
  waiting for transfers between devices: 490 us -> 247 us
  starting transfers between devices: 2.94 us -> 36 us
  local copies, waits for them, and re-layouts: 4.29 us -> 25.1 us
  between operations: 15.1 us -> 2.45 us
  other arithmetic: 12.1 us -> 3.18 us
  matrix products: 15.6 us -> 23.3 us
    all_gather x2 -> x0, waiting for transfers between devices: 340 us -> none  [gradient(): lax.all_gather(tok_rows, 'shard', axis=0, tiled=True)]
    ppermute x0 -> x20, waiting for transfers between devices: none -> 110 us  [the longest x18 110 us: shifted(): return lax.ppermute(block, axis, [(i, route_of(i)) for i in range(count)])]
    ppermute x0 -> x20, starting transfers between devices: none -> 31.8 us  [the longest x18 21.5 us: shifted(): return lax.ppermute(block, axis, [(i, route_of(i)) for i in range(count)])]
    unnamed x6 -> x50, local copies, waits for them, and re-layouts: 0.64 us -> 17.7 us
    reduce_scatter x2 -> x0, waiting for transfers between devices: 11.4 us -> none  [gradient(): return lax.psum_scatter(summed, 'dp', scatter_dimension=0, tiled=True)]
    dot_general x2 -> x4, matrix products: 15.6 us -> 23.3 us  [the longest x2 15.1 us: gradient(): lax.dot_general(mine, cot_rel, dims, preferred_element_type=jnp.float32)]
    broadcast_in_dim x2 -> x1, other arithmetic: 9.44 us -> 3.18 us  [local(): return (params_now[None], moment_now[None])]
  transfers between devices with their start and end apart: 6 -> 22, of which waited for: 5 -> 9; matrix products, arithmetic and copies ran while one was open for 3% -> 11% of each run, Pallas kernels for 0% -> 0%
where the time goes in v1:
time: 338 us; the launch traced here: 337 us
  waiting for transfers between devices  247 us (73%)
  starting transfers between devices  36 us (11%)
  local copies, waits for them, and re-layouts  25.1 us (7%)
  matrix products  23.3 us (7%)
    ppermute x2, waiting for transfers between devices, swapped(): return lax.ppermute(block, axis, route)  137 us
    ppermute x18, waiting for transfers between devices, shifted(): return lax.ppermute(block, axis, [(i, route_of(i)) for i in range(count)])  110 us
    ppermute x18, starting transfers between devices, shifted(): return lax.ppermute(block, axis, [(i, route_of(i)) for i in range(count)])  21.5 us
    unnamed x50, local copies, waits for them, and re-layouts  17.7 us
    dot_general x2, matrix products, gradient(): lax.dot_general(mine, cot_rel, dims, preferred_element_type=jnp.float32)  15.1 us
    ppermute x2, starting transfers between devices, gradient(): sent = lax.ppermute(part_other, 'dp', [(0, 1), (1, 0)])  10.3 us
    dot_general x2, matrix products, gradient(): lax.dot_general(other, cot_rel, dims, preferred_element_type=jnp.float32)  8.19 us
  transfers between devices with their start and end apart: 22, of which 9 were waited for; matrix products, arithmetic and copies ran while one was open for 11% of the time, Pallas kernels for 0%

profile of v1, /device:TPU:1, one launch (start us, length us, event | category | flops | bytes accessed | tf_op | source)
XLA Modules:
  0.0 337.3 jit_solution(1700805661624116155)
XLA Ops:
  0.6 3.2 slice_bitcast_fusion.1
  3.9 2.5 collective-permute-start.12
  6.3 1.3 collective-permute-start.13
  7.6 1.4 collective-permute-start.15
  9.1 1.4 constant_dynamic-update-slice_fusion.9
  10.6 0.2 copy-done.4
  11.3 17.2 %collective-permute-done.12 = bf16[128,4096]{1,0:T(8,128)(2,1)} collective-permute-done((bf16[128,4096]{1,0:T(8,128)(2,1)}, bf16[128,4096]{1,0:T(8,128)(2,1)}, u32[]{:S(2)}, u32[]{:S(2)}) %collective-permute-start.12) | collective-permute-done | bytes 1048608 | tf_op jit(solution)/shard_map/ppermute | solution.py:27
  28.5 3.6 %collective-permute-start.25 = (bf16[128,4096]{1,0:T(8,128)(2,1)}, bf16[128,4096]{1,0:T(8,128)(2,1)S(1)}, u32[]{:S(2)}, u32[]{:S(2)}) collective-permute-start(bf16[128,4096]{1,0:T(8,128)(2,1)} %get-tuple-element.23), channel_id=1, source_target_pairs={{0,6},{1,7},{2,0},{3,1},{4,2},{5,3},{6,4},{7,5},{8,14},{9,15},{10,... | collective-permute-start | bytes 3145736 | tf_op jit(solution)/shard_map/ppermute | solution.py:27
  32.1 2.3 constant_dynamic-update-slice_fusion.8
  34.4 2.3 constant_dynamic-update-slice_fusion.7
  36.7 1.2 slice.68
  38.1 12.8 %collective-permute-done.22 = bf16[128,4096]{1,0:T(8,128)(2,1)} collective-permute-done((bf16[128,4096]{1,0:T(8,128)(2,1)}, bf16[128,4096]{1,0:T(8,128)(2,1)}, u32[]{:S(2)}, u32[]{:S(2)}) %collective-permute-start.22) | collective-permute-done | bytes 1048608 | tf_op jit(solution)/shard_map/ppermute | solution.py:27
  50.9 3.6 %collective-permute-start.18 = (bf16[64,4096]{1,0:T(8,128)(2,1)S(1)}, bf16[64,4096]{1,0:T(8,128)(2,1)S(1)}, u32[]{:S(2)}, u32[]{:S(2)}) collective-permute-start(bf16[64,4096]{1,0:T(8,128)(2,1)S(1)} %slice.69), channel_id=1, source_target_pairs={{0,6},{1,7},{2,0},{3,1},{4,2},{5,3},{6,4},{7,5},{8,14},{9,15},{10,... | collective-permute-start | bytes 1572872 | tf_op jit(solution)/shard_map/ppermute | solution.py:27
  54.6 2.3 constant_dynamic-update-slice_fusion.26
  56.9 2.3 constant_dynamic-update-slice_fusion.25
  59.2 1.1 slice.72
  60.4 16.2 %collective-permute-done.14 = bf16[128,4096]{1,0:T(8,128)(2,1)S(1)} collective-permute-done((bf16[128,4096]{1,0:T(8,128)(2,1)}, bf16[128,4096]{1,0:T(8,128)(2,1)S(1)}, u32[]{:S(2)}, u32[]{:S(2)}) %collective-permute-start.14) | collective-permute-done | bytes 1048608 | tf_op jit(solution)/shard_map/ppermute | solution.py:27
  76.6 1.3 collective-permute-start.16
  78.1 32.2 %collective-permute-done.24 = bf16[128,4096]{1,0:T(8,128)(2,1)S(1)} collective-permute-done((bf16[128,4096]{1,0:T(8,128)(2,1)}, bf16[128,4096]{1,0:T(8,128)(2,1)S(1)}, u32[]{:S(2)}, u32[]{:S(2)}) %collective-permute-start.24) | collective-permute-done | bytes 1048608 | tf_op jit(solution)/shard_map/ppermute | solution.py:27
  110.3 1.3 collective-permute-start.26
  111.7 1.1 constant_dynamic-update-slice_fusion.24
  112.8 1.0 constant_dynamic-update-slice_fusion.23
  113.8 0.5 collective-permute-start.28
  114.4 17.8 %collective-permute-done.26 = bf16[128,4096]{1,0:T(8,128)(2,1)S(1)} collective-permute-done((bf16[128,4096]{1,0:T(8,128)(2,1)}, bf16[128,4096]{1,0:T(8,128)(2,1)S(1)}, u32[]{:S(2)}, u32[]{:S(2)}) %collective-permute-start.26) | collective-permute-done | bytes 1048608 | tf_op jit(solution)/shard_map/ppermute | solution.py:27
  132.2 1.0 constant_dynamic-update-slice_fusion.22
  133.3 2.8 collective-permute-start.20
  136.4 2.7 collective-permute-start.30
  139.1 0.8 constant_dynamic-update-slice_fusion.21
  139.9 3.5 %collective-permute-done.28 = bf16[64,4096]{1,0:T(8,128)(2,1)S(1)} collective-permute-done((bf16[64,4096]{1,0:T(8,128)(2,1)S(1)}, bf16[64,4096]{1,0:T(8,128)(2,1)S(1)}, u32[]{:S(2)}, u32[]{:S(2)}) %collective-permute-start.28) | collective-permute-done | bytes 524320 | tf_op jit(solution)/shard_map/ppermute | solution.py:27
  143.5 0.8 constant_dynamic-update-slice_fusion.20
  144.3 10.4 %collective-permute-done.20 = bf16[64,4096]{1,0:T(8,128)(2,1)S(1)} collective-permute-done((bf16[64,4096]{1,0:T(8,128)(2,1)S(1)}, bf16[64,4096]{1,0:T(8,128)(2,1)S(1)}, u32[]{:S(2)}, u32[]{:S(2)}) %collective-permute-start.20) | collective-permute-done | bytes 524320 | tf_op jit(solution)/shard_map/ppermute | solution.py:27
  154.8 3.2 fusion.4
  158.0 0.7 copy-done.3
  158.7 7.4 %collective-permute-start.21 = (f32[2048,256]{1,0:T(8,128)}, f32[2048,256]{1,0:T(8,128)}, u32[]{:S(2)}, u32[]{:S(2)}) collective-permute-start(f32[2048,256]{1,0:T(8,128)} %fusion.4), channel_id=1, source_target_pairs={{0,8},{8,0},{1,9},{9,1},{2,10},{10,2},{3,11},{11,3},{4,12},{12,4},... | collective-permute-start | bytes 6291464 | tf_op jit(solution)/shard_map/ppermute | solution.py:81
  166.1 0.8 constant_dynamic-update-slice_fusion.19
  166.9 0.8 constant_dynamic-update-slice_fusion.18
  167.8 5.0 %fusion = f32[2048,256]{1,0:T(8,128)} fusion(bf16[1024,256]{1,0:T(8,128)(2,1)S(1)} %copy-done.8, bf16[1024,4096]{1,0:T(8,128)(2,1)} %constant_dynamic-update-slice_fusion.18, s32[]{:T(128)S(6)} %select_n.106), kind=kOutput, calls=%fused_computation.2 | convolution fusion | flops 1073741824 | bytes 6815748 | tf_op jit(solution)/shard_map/dot_general | solution.py:80
  172.7 2.9 collective-permute-start.31
  175.7 0.7 fusion.24
  177.7 6.5 %bitcast_subtract_fusion = (f32[2048,256]{1,0:T(8,128)S(1)}, f32[2048,256]{1,0:T(8,128)}) fusion(f32[1,2048,256]{2,1,0:T(8,128)S(1)} %copy-done, f32[1,2048,256]{2,1,0:T(8,128)} %param.15, f32[2048,256]{1,0:T(8,128)} %collective-permute-done.21, bf16[1024,256]{1,0:T(8,128)(2,1)S(1)} %copy-done.6, bf16[1024,4096]{1,0:T(8,128)(2,1)} %copy-done.3, ...), kind=kOutput, calls=%fused_computation.14 | convolution fusion | flops 1077411840 | bytes 15204356 | tf_op jit(solution)/shard_map/dot_general | solution.py:82
  184.2 47.3 %conditional.2 = (f32[2048,256]{1,0:T(8,128)}) conditional(s32[]{:T(128)} %clamp.6, f32[2048,256]{1,0:T(8,128)S(1)} %get-tuple-element.30, f32[2048,256]{1,0:T(8,128)S(1)} %get-tuple-element.30, f32[2048,256]{1,0:T(8,128)S(1)} %get-tuple-element.30), branch_computations={%region_0.1_spmd, %region_1.2_spmd, %region_2.3_spmd} | conditional | flops 524288 | bytes 25165992 | solution.py:112
  184.2 1.2 collective-permute-start
  185.4 46.1 %collective-permute-done = f32[2048,256]{1,0:T(8,128)} collective-permute-done((f32[2048,256]{1,0:T(8,128)S(1)}, f32[2048,256]{1,0:T(8,128)}, u32[]{:S(2)}, u32[]{:S(2)}) %collective-permute-start) | collective-permute-done | bytes 2097184 | tf_op jit(solution)/shard_map/cond/branch_0_fun/ppermute | solution.py:22
  231.5 8.6 %fusion.16 = (f32[1,2048,256]{2,1,0:T(8,128)}, f32[2048,256]{1,0:T(8,128)S(1)}) fusion(f32[2048,256]{1,0:T(8,128)} %get-tuple-element.31, f32[1,2048,256]{2,1,0:T(8,128)} %param.15, f32[2048,256]{1,0:T(8,128)} %get-tuple-element.34, f32[1,2048,256]{2,1,0:T(8,128)} %param.14, f32[2048,256]{1,0:T(8,128)} %collective-permute-done.31, ...), kind=kOutput, calls=%fused_computation.20 | convolution fusion | flops 1081081856 | bytes 19398660 | tf_op jit(solution)/shard_map/dot_general | solution.py:82
  240.1 94.0 %conditional.3 = (f32[2048,256]{1,0:T(8,128)}) conditional(s32[]{:T(128)} %clamp.7, f32[2048,256]{1,0:T(8,128)S(1)} %get-tuple-element.21, f32[2048,256]{1,0:T(8,128)S(1)} %get-tuple-element.21, f32[2048,256]{1,0:T(8,128)S(1)} %get-tuple-element.21), branch_computations={%region_3.4_spmd, %region_4.5_spmd, %region_5.6_spmd} | conditional | flops 524288 | bytes 25165992 | solution.py:112
  240.1 3.0 collective-permute-start.3
  243.1 91.0 %collective-permute-done.3 = f32[2048,256]{1,0:T(8,128)} collective-permute-done((f32[2048,256]{1,0:T(8,128)S(1)}, f32[2048,256]{1,0:T(8,128)}, u32[]{:S(2)}, u32[]{:S(2)}) %collective-permute-start.3) | collective-permute-done | bytes 2097184 | tf_op jit(solution)/shard_map/cond/branch_2_fun/ppermute | solution.py:22
  334.1 3.2 multiply_bitcast_fusion
  (68 shorter events, 1.3 us)
Async XLA Ops:
  0.6 8.5 %copy-start.1 = (bf16[2,1,128,4096]{3,2,1,0:T(8,128)(2,1)S(1)}, bf16[2,1,128,4096]{3,2,1,0:T(8,128)(2,1)}, u32[]{:S(2)}) copy-start(bf16[2,1,128,4096]{3,2,1,0:T(8,128)(2,1)} %param.12) | copy-start | bytes 6291460
  3.9 24.6 %collective-permute-start.12 = (bf16[128,4096]{1,0:T(8,128)(2,1)}, bf16[128,4096]{1,0:T(8,128)(2,1)}, u32[]{:S(2)}, u32[]{:S(2)}) collective-permute-start(bf16[128,4096]{1,0:T(8,128)(2,1)} %get-tuple-element.22), channel_id=1, source_target_pairs={{0,1},{1,0},{2,3},{3,2},{4,5},{5,4},{6,7},{7,6},{8,9},{9,8},{10,11... | collective-permute-start | bytes 3145736 | tf_op jit(solution)/shard_map/ppermute | solution.py:27
  6.3 28.1 %collective-permute-start.13 = (bf16[128,4096]{1,0:T(8,128)(2,1)}, bf16[128,4096]{1,0:T(8,128)(2,1)}, u32[]{:S(2)}, u32[]{:S(2)}) collective-permute-start(bf16[128,4096]{1,0:T(8,128)(2,1)} %get-tuple-element.22), channel_id=1, source_target_pairs={{0,2},{1,3},{2,4},{3,5},{4,6},{5,7},{6,0},{7,1},{8,10},{9,11},{10,... | collective-permute-start | bytes 3145736 | tf_op jit(solution)/shard_map/ppermute | solution.py:27
  7.6 30.3 %collective-permute-start.15 = (bf16[128,4096]{1,0:T(8,128)(2,1)}, bf16[128,4096]{1,0:T(8,128)(2,1)S(1)}, u32[]{:S(2)}, u32[]{:S(2)}) collective-permute-start(bf16[128,4096]{1,0:T(8,128)(2,1)} %get-tuple-element.22), channel_id=1, source_target_pairs={{0,6},{1,7},{2,0},{3,1},{4,2},{5,3},{6,4},{7,5},{8,14},{9,15},{10,... | collective-permute-start | bytes 3145736 | tf_op jit(solution)/shard_map/ppermute | solution.py:27
  9.1 41.9 %collective-permute-start.22 = (bf16[128,4096]{1,0:T(8,128)(2,1)}, bf16[128,4096]{1,0:T(8,128)(2,1)}, u32[]{:S(2)}, u32[]{:S(2)}) collective-permute-start(bf16[128,4096]{1,0:T(8,128)(2,1)} %get-tuple-element.23), channel_id=1, source_target_pairs={{0,1},{1,0},{2,3},{3,2},{4,5},{5,4},{6,7},{7,6},{8,9},{9,8},{10,11... | collective-permute-start | bytes 3145736 | tf_op jit(solution)/shard_map/ppermute | solution.py:27
  9.1 47.7 %collective-permute-start.23 = (bf16[128,4096]{1,0:T(8,128)(2,1)}, bf16[128,4096]{1,0:T(8,128)(2,1)}, u32[]{:S(2)}, u32[]{:S(2)}) collective-permute-start(bf16[128,4096]{1,0:T(8,128)(2,1)} %get-tuple-element.23), channel_id=1, source_target_pairs={{0,2},{1,3},{2,4},{3,5},{4,6},{5,7},{6,0},{7,1},{8,10},{9,11},{10,... | collective-permute-start | bytes 3145736 | tf_op jit(solution)/shard_map/ppermute | solution.py:27
  9.1 1.6 copy-start.4
  11.2 143.5 %copy-start.5 = (bf16[1024,256]{1,0:T(8,128)(2,1)}, bf16[1024,256]{1,0:T(8,128)(2,1)S(1)}, u32[]{:S(2)}) copy-start(bf16[1024,256]{1,0:T(8,128)(2,1)S(1)} %constant_dynamic-update-slice_fusion.10) | copy-start | bytes 1572868
  11.3 45.6 %copy-start.7 = (bf16[1024,256]{1,0:T(8,128)(2,1)}, bf16[1024,256]{1,0:T(8,128)(2,1)S(1)}, u32[]{:S(2)}) copy-start(bf16[1024,256]{1,0:T(8,128)(2,1)S(1)} %constant_dynamic-update-slice_fusion.28) | copy-start | bytes 1572868
  28.5 31.8 %collective-permute-start.25 = (bf16[128,4096]{1,0:T(8,128)(2,1)}, bf16[128,4096]{1,0:T(8,128)(2,1)S(1)}, u32[]{:S(2)}, u32[]{:S(2)}) collective-permute-start(bf16[128,4096]{1,0:T(8,128)(2,1)} %get-tuple-element.23), channel_id=1, source_target_pairs={{0,6},{1,7},{2,0},{3,1},{4,2},{5,3},{6,4},{7,5},{8,14},{9,15},{10,... | collective-permute-start | bytes 3145736 | tf_op jit(solution)/shard_map/ppermute | solution.py:27
  34.4 42.2 %collective-permute-start.14 = (bf16[128,4096]{1,0:T(8,128)(2,1)}, bf16[128,4096]{1,0:T(8,128)(2,1)S(1)}, u32[]{:S(2)}, u32[]{:S(2)}) collective-permute-start(bf16[128,4096]{1,0:T(8,128)(2,1)} %collective-permute-done.12), channel_id=1, source_target_pairs={{0,2},{1,3},{2,4},{3,5},{4,6},{5,7},{6,0},{7,1},{8,10},{9,11},{10,... | collective-permute-start | bytes 3145736 | tf_op jit(solution)/shard_map/ppermute | solution.py:27
  36.7 41.3 %copy-start.2 = (bf16[1024,4096]{1,0:T(8,128)(2,1)S(1)}, bf16[1024,4096]{1,0:T(8,128)(2,1)}, u32[]{:S(2)}) copy-start(bf16[1024,4096]{1,0:T(8,128)(2,1)} %constant_dynamic-update-slice_fusion.7) | copy-start | bytes 25165828
  38.0 95.4 %collective-permute-start.17 = (bf16[64,4096]{1,0:T(8,128)(2,1)S(1)}, bf16[64,4096]{1,0:T(8,128)(2,1)S(1)}, u32[]{:S(2)}, u32[]{:S(2)}) collective-permute-start(bf16[64,4096]{1,0:T(8,128)(2,1)S(1)} %slice.68), channel_id=1, source_target_pairs={{0,2},{1,3},{2,4},{3,5},{4,6},{5,7},{6,0},{7,1},{8,10},{9,11},{10,... | collective-permute-start | bytes 1572872 | tf_op jit(solution)/shard_map/ppermute | solution.py:27
  50.9 85.2 %collective-permute-start.18 = (bf16[64,4096]{1,0:T(8,128)(2,1)S(1)}, bf16[64,4096]{1,0:T(8,128)(2,1)S(1)}, u32[]{:S(2)}, u32[]{:S(2)}) collective-permute-start(bf16[64,4096]{1,0:T(8,128)(2,1)S(1)} %slice.69), channel_id=1, source_target_pairs={{0,6},{1,7},{2,0},{3,1},{4,2},{5,3},{6,4},{7,5},{8,14},{9,15},{10,... | collective-permute-start | bytes 1572872 | tf_op jit(solution)/shard_map/ppermute | solution.py:27
  56.9 53.5 %collective-permute-start.24 = (bf16[128,4096]{1,0:T(8,128)(2,1)}, bf16[128,4096]{1,0:T(8,128)(2,1)S(1)}, u32[]{:S(2)}, u32[]{:S(2)}) collective-permute-start(bf16[128,4096]{1,0:T(8,128)(2,1)} %collective-permute-done.22), channel_id=1, source_target_pairs={{0,2},{1,3},{2,4},{3,5},{4,6},{5,7},{6,0},{7,1},{8,10},{9,11},{10,... | collective-permute-start | bytes 3145736 | tf_op jit(solution)/shard_map/ppermute | solution.py:27
  60.3 76.1 %collective-permute-start.27 = (bf16[64,4096]{1,0:T(8,128)(2,1)S(1)}, bf16[64,4096]{1,0:T(8,128)(2,1)S(1)}, u32[]{:S(2)}, u32[]{:S(2)}) collective-permute-start(bf16[64,4096]{1,0:T(8,128)(2,1)S(1)} %slice.72), channel_id=1, source_target_pairs={{0,2},{1,3},{2,4},{3,5},{4,6},{5,7},{6,0},{7,1},{8,10},{9,11},{10,... | collective-permute-start | bytes 1572872 | tf_op jit(solution)/shard_map/ppermute | solution.py:27
  76.6 37.2 %collective-permute-start.16 = (bf16[128,4096]{1,0:T(8,128)(2,1)}, bf16[128,4096]{1,0:T(8,128)(2,1)S(1)}, u32[]{:S(2)}, u32[]{:S(2)}) collective-permute-start(bf16[128,4096]{1,0:T(8,128)(2,1)} %collective-permute-done.12), channel_id=1, source_target_pairs={{0,6},{1,7},{2,0},{3,1},{4,2},{5,3},{6,4},{7,5},{8,14},{9,15},{10,... | collective-permute-start | bytes 3145736 | tf_op jit(solution)/shard_map/ppermute | solution.py:27
  110.3 21.9 %collective-permute-start.26 = (bf16[128,4096]{1,0:T(8,128)(2,1)}, bf16[128,4096]{1,0:T(8,128)(2,1)S(1)}, u32[]{:S(2)}, u32[]{:S(2)}) collective-permute-start(bf16[128,4096]{1,0:T(8,128)(2,1)} %collective-permute-done.22), channel_id=1, source_target_pairs={{0,6},{1,7},{2,0},{3,1},{4,2},{5,3},{6,4},{7,5},{8,14},{9,15},{10,... | collective-permute-start | bytes 3145736 | tf_op jit(solution)/shard_map/ppermute | solution.py:27
  113.8 29.6 %collective-permute-start.28 = (bf16[64,4096]{1,0:T(8,128)(2,1)S(1)}, bf16[64,4096]{1,0:T(8,128)(2,1)S(1)}, u32[]{:S(2)}, u32[]{:S(2)}) collective-permute-start(bf16[64,4096]{1,0:T(8,128)(2,1)S(1)} %slice.73), channel_id=1, source_target_pairs={{0,6},{1,7},{2,0},{3,1},{4,2},{5,3},{6,4},{7,5},{8,14},{9,15},{10,... | collective-permute-start | bytes 1572872 | tf_op jit(solution)/shard_map/ppermute | solution.py:27
  132.2 12.1 %collective-permute-start.19 = (bf16[64,4096]{1,0:T(8,128)(2,1)S(1)}, bf16[64,4096]{1,0:T(8,128)(2,1)S(1)}, u32[]{:S(2)}, u32[]{:S(2)}) collective-permute-start(bf16[64,4096]{1,0:T(8,128)(2,1)S(1)} %slice.70), channel_id=1, source_target_pairs={{0,2},{1,3},{2,4},{3,5},{4,6},{5,7},{6,0},{7,1},{8,10},{9,11},{10,... | collective-permute-start | bytes 1572872 | tf_op jit(solution)/shard_map/ppermute | solution.py:27
  133.3 21.4 %collective-permute-start.20 = (bf16[64,4096]{1,0:T(8,128)(2,1)S(1)}, bf16[64,4096]{1,0:T(8,128)(2,1)S(1)}, u32[]{:S(2)}, u32[]{:S(2)}) collective-permute-start(bf16[64,4096]{1,0:T(8,128)(2,1)S(1)} %slice.71), channel_id=1, source_target_pairs={{0,6},{1,7},{2,0},{3,1},{4,2},{5,3},{6,4},{7,5},{8,14},{9,15},{10,... | collective-permute-start | bytes 1572872 | tf_op jit(solution)/shard_map/ppermute | solution.py:27
  136.2 29.9 %collective-permute-start.29 = (bf16[64,4096]{1,0:T(8,128)(2,1)S(1)}, bf16[64,4096]{1,0:T(8,128)(2,1)S(1)}, u32[]{:S(2)}, u32[]{:S(2)}) collective-permute-start(bf16[64,4096]{1,0:T(8,128)(2,1)S(1)} %slice.74), channel_id=1, source_target_pairs={{0,2},{1,3},{2,4},{3,5},{4,6},{5,7},{6,0},{7,1},{8,10},{9,11},{10,... | collective-permute-start | bytes 1572872 | tf_op jit(solution)/shard_map/ppermute | solution.py:27
  136.4 30.5 %collective-permute-start.30 = (bf16[64,4096]{1,0:T(8,128)(2,1)S(1)}, bf16[64,4096]{1,0:T(8,128)(2,1)S(1)}, u32[]{:S(2)}, u32[]{:S(2)}) collective-permute-start(bf16[64,4096]{1,0:T(8,128)(2,1)S(1)} %slice.75), channel_id=1, source_target_pairs={{0,6},{1,7},{2,0},{3,1},{4,2},{5,3},{6,4},{7,5},{8,14},{9,15},{10,... | collective-permute-start | bytes 1572872 | tf_op jit(solution)/shard_map/ppermute | solution.py:27
  154.8 3.9 %copy-start.3 = (bf16[1024,4096]{1,0:T(8,128)(2,1)}, bf16[1024,4096]{1,0:T(8,128)(2,1)S(1)}, u32[]{:S(2)}) copy-start(bf16[1024,4096]{1,0:T(8,128)(2,1)S(1)} %constant_dynamic-update-slice_fusion) | copy-start | bytes 25165828
  154.8 13.0 %copy-start.8 = (bf16[1024,256]{1,0:T(8,128)(2,1)S(1)}, bf16[1024,256]{1,0:T(8,128)(2,1)}, u32[]{:S(2)}) copy-start(bf16[1024,256]{1,0:T(8,128)(2,1)} %copy-done.7) | copy-start | bytes 1572868
  158.7 19.0 %collective-permute-start.21 = (f32[2048,256]{1,0:T(8,128)}, f32[2048,256]{1,0:T(8,128)}, u32[]{:S(2)}, u32[]{:S(2)}) collective-permute-start(f32[2048,256]{1,0:T(8,128)} %fusion.4), channel_id=1, source_target_pairs={{0,8},{8,0},{1,9},{9,1},{2,10},{10,2},{3,11},{11,3},{4,12},{12,4},... | collective-permute-start | bytes 6291464 | tf_op jit(solution)/shard_map/ppermute | solution.py:81
  167.7 7.9 %copy-start.9 = (s32[2]{0:T(128)S(1)}, s32[2]{0:T(128)}, u32[]{:S(2)}) copy-start(s32[2]{0:T(128)} %param.11) | copy-start | bytes 28
  167.7 9.9 %copy-start = (f32[1,2048,256]{2,1,0:T(8,128)S(1)}, f32[1,2048,256]{2,1,0:T(8,128)}, u32[]{:S(2)}) copy-start(f32[1,2048,256]{2,1,0:T(8,128)} %param.14) | copy-start | bytes 6291460
  167.8 9.9 %copy-start.6 = (bf16[1024,256]{1,0:T(8,128)(2,1)S(1)}, bf16[1024,256]{1,0:T(8,128)(2,1)}, u32[]{:S(2)}) copy-start(bf16[1024,256]{1,0:T(8,128)(2,1)} %copy-done.5) | copy-start | bytes 1572868
  172.7 58.8 %collective-permute-start.31 = (f32[2048,256]{1,0:T(8,128)}, f32[2048,256]{1,0:T(8,128)}, u32[]{:S(2)}, u32[]{:S(2)}) collective-permute-start(f32[2048,256]{1,0:T(8,128)} %fusion), channel_id=1, source_target_pairs={{0,8},{8,0},{1,9},{9,1},{2,10},{10,2},{3,11},{11,3},{4,12},{12,4},... | collective-permute-start | bytes 6291464 | tf_op jit(solution)/shard_map/ppermute | solution.py:81
  184.2 47.3 %collective-permute-start = (f32[2048,256]{1,0:T(8,128)S(1)}, f32[2048,256]{1,0:T(8,128)}, u32[]{:S(2)}, u32[]{:S(2)}) collective-permute-start(f32[2048,256]{1,0:T(8,128)S(1)} %param), channel_id=1, source_target_pairs={{0,16},{16,0},{32,48},{48,32},{64,80},{80,64},{96,112},{112,96},{1... | collective-permute-start | bytes 6291464 | tf_op jit(solution)/shard_map/cond/branch_0_fun/ppermute | solution.py:22
  240.1 94.0 %collective-permute-start.3 = (f32[2048,256]{1,0:T(8,128)S(1)}, f32[2048,256]{1,0:T(8,128)}, u32[]{:S(2)}, u32[]{:S(2)}) collective-permute-start(f32[2048,256]{1,0:T(8,128)S(1)} %param.5), channel_id=1, source_target_pairs={{0,64},{64,0},{16,80},{80,16},{32,96},{96,32},{48,112},{112,48},{1... | collective-permute-start | bytes 6291464 | tf_op jit(solution)/shard_map/cond/branch_2_fun/ppermute | solution.py:22
